TPU v7x, 256 devices: a whole 4x4x8 slice. The times are simulated.
256 devices in a mesh: dp: 8 (over z), ctx: 32 (over x, y, core).
Axes of the slice: x: 4, y: 4, z: 8, core: 2. Of those that a mesh axis runs over, the one named last changes fastest.
Arguments:
- head_inputs: bfloat16 [8, 4096, 2048], P('dp', 'ctx'), may hold values from -11 to 11
- entry_operator: bfloat16 [8, 4096, 128], P('dp', 'ctx'), may hold values from -3 to 3
- memory_readout: bfloat16 [8, 4096, 128], P('dp', 'ctx'), may hold values from -0.1796875 to 0.1796875
- unshifted_strides: float32 [8, 64, 4096], P('dp', None, 'ctx'), may hold values from -1.5 to 5.5, as said below
- log_decay_rates: float32 [64], P('dp'), may hold values from -11 to -2
- stride_shift: float32 [64], P('dp'), may hold values from -0.5 to 0.5
- bypass_coefficients: float32 [64], P('dp'), may hold values from 0.5 to 1.5
- result_cotangent: bfloat16 [8, 4096, 2048], P('dp', 'ctx'), may hold values from -26 to 26
Outputs:
- output: bfloat16 [8, 4096, 2048], P('dp', 'ctx')
- channels_grad: bfloat16 [8, 4096, 2048], P('dp', 'ctx')
- input_map_grad: float32 [8, 4096, 128], P('dp', 'ctx')
- output_map_grad: float32 [8, 4096, 128], P('dp', 'ctx')
- timestep_raw_gradient: float32 [8, 64, 4096], P('dp', None, 'ctx')
- a_log_grad: float32 [64], P('dp')
- bias_grad: float32 [64], P('dp')
- skip_grad: float32 [64], P('dp')
Inputs may be any that keep to these rules, and one draw needn't show every extreme that they name: `unshifted_strides`: step sizes are moderate at most positions, with a few large ones in each sequence.
All inputs are finite; a program needn't handle non-finite values.
Results may differ from a plain program's by a relative error of at most 0.001.
Values sent between devices are 32-bit elements; how exact they have to be, the bound alone decides.
A program may use at most 128 MiB of HBM per device.

v0:
```python
import jax
import jax.numpy as jnp
from jax import lax
from jax.sharding import Mesh
from jax.sharding import PartitionSpec as P

CTX = ("ctx_0", "ctx_1", "ctx_2")
maximal_accuracy = lax.Precision.HIGHEST


def rows_first(arrays, axis, dims):
    turned = [jnp.moveaxis(a, dim, 0) for a, dim in zip(arrays, dims)]
    widths = [t[0].size for t in turned]
    both = jnp.concatenate([t.reshape(-1, w) for t, w in zip(turned, widths)], axis=1)
    result = lax.all_gather(both, axis, axis=0, tiled=True)
    tiles = jnp.split(result, [sum(widths[:k]) for k in range(1, len(widths))], axis=1)
    return tuple(
        (
            jnp.moveaxis(b.reshape(-1, *t.shape[1:]), 0, dim)
            for b, t, dim in zip(tiles, turned, dims)
        )
    )


def nothing_yet(array, identity):
    return jax.tree.map(
        lambda a, e: jnp.broadcast_to(jnp.asarray(e, a.dtype), a.shape), array, identity
    )


def entering(array, axes, combine, identity, reverse):
    before = start = nothing_yet(array, identity)
    subtotal = array
    for axis in reversed(axes):
        devices, position = (lax.axis_size(axis), lax.axis_index(axis))
        pieces = jax.tree.map(lambda part: lax.all_gather(part, axis), subtotal)
        inside, subtotal = (start, start)
        for k in reversed(range(devices)) if reverse else range(devices):
            passed = k > position if reverse else k < position
            subtotal = combine(subtotal, jax.tree.map(lambda part: part[k], pieces))
            inside = jax.tree.map(lambda new, old: jnp.where(passed, new, old), subtotal, inside)
        before = combine(inside, before)
    return before


def split_up(array, dim, devices):
    dims = array.shape
    tiles = array.reshape(*dims[:dim], devices, dims[dim] // devices, *dims[dim + 1 :])
    return jnp.moveaxis(tiles, dim, 0)


def summed_on_arrival(array, axis, dim):
    devices = lax.axis_size(axis)
    tiles = lax.all_to_all(split_up(array, dim, devices), axis, 0, 0, tiled=True)
    return jnp.sum(tiles, axis=0)


def copy_for_each(array, axis):
    devices = lax.axis_size(axis)
    return lax.all_to_all(
        jnp.broadcast_to(array[None], (devices, *array.shape)), axis, 0, 0, tiled=True
    )


def of_everyone(array, axis):
    everything = copy_for_each(array, axis)
    return jnp.sum(everything, axis=0)


def packed_total(arrays, axis):
    vector, at, gathered = (jnp.concatenate([a.reshape(-1) for a in arrays]), 0, [])
    subtotal = of_everyone(vector, axis)
    for a in arrays:
        gathered.append(subtotal[at : at + a.size].reshape(a.shape))
        at += a.size
    return tuple(gathered)


def local_part(xg, write_operator, gram, dtr, rate_log, bias, skip):
    count = xg.shape[0]
    heads = dtr.shape[0]
    xg3 = xg.reshape(count, heads, -1)
    step = jax.nn.softplus(dtr + bias[:, None])
    logdecay = -jnp.exp(rate_log)[:, None] * step
    cum = jnp.cumsum(logdecay, axis=1)
    rows = lax.broadcasted_iota(jnp.int32, (count, count), 0)
    cols = lax.broadcasted_iota(jnp.int32, (count, count), 1)
    diff = cum[:, :, None] - cum[:, None, :]
    seg = jnp.exp(jnp.where((rows >= cols)[None], diff, -jnp.inf))
    weights = gram[None] * seg * step[:, None, :]
    inner = jnp.einsum("hts,shp->thp", weights, xg3, precision=maximal_accuracy)
    y_part = inner + skip[None, :, None] * xg3
    tail = jnp.exp(cum[:, -1:] - cum) * step
    scaled = xg3 * tail.T[:, :, None]
    state = jnp.einsum("shp,sn->hpn", scaled, write_operator, precision=maximal_accuracy)
    return (y_part, state, jnp.exp(cum))


def combine(earlier, later):
    return (earlier[0] * later[0], later[0][:, None, None] * earlier[1] + later[1])


def local(
    head_inputs,
    entry_operator,
    memory_readout,
    unshifted_strides,
    log_decay_rates,
    stride_shift,
    bypass_coefficients,
    result_cotangent,
):
    rate_all, full_bias_vector, skip_all = rows_first(
        (log_decay_rates, stride_shift, bypass_coefficients), "dp", (0, 0, 0)
    )
    tokens = head_inputs[0].astype(jnp.float32)
    write_operator = entry_operator[0].astype(jnp.float32)
    cmat = memory_readout[0].astype(jnp.float32)
    gram = lax.dot_general(
        memory_readout[0],
        entry_operator[0],
        (((1,), (1,)), ((), ())),
        preferred_element_type=jnp.float32,
    )
    raw = unshifted_strides[0]
    upstream = result_cotangent[0].astype(jnp.float32)
    heads = raw.shape[0]
    width = tokens.shape[1] // heads
    count = tokens.shape[0]
    parts = 1
    per = heads // parts
    output_pieces, dx_list, dt_list, rate_list, bias_list, skip_list = ([], [], [], [], [], [])
    cmat_grad = jnp.zeros_like(cmat)
    (y_part, state, growth_factor), backward = jax.vjp(
        local_part, tokens, write_operator, gram, raw, rate_all, full_bias_vector, skip_all
    )
    ends = growth_factor[:, -1]
    identity = (jnp.ones_like(ends), jnp.zeros_like(state))
    _, carried = entering((ends, state), CTX, combine, identity, False)
    readout = jnp.einsum("tn,hpn->thp", cmat, carried, precision=maximal_accuracy)
    output_pieces.append(y_part + growth_factor.T[:, :, None] * readout)
    g_group = upstream.reshape(count, per, width)
    dread = growth_factor.T[:, :, None] * g_group
    growth_grad = jnp.einsum("thp,thp->ht", g_group, readout, precision=maximal_accuracy)
    local_grad = jnp.einsum("thp,tn->hpn", dread, cmat, precision=maximal_accuracy)
    cmat_grad = cmat_grad + jnp.einsum("thp,hpn->tn", dread, carried, precision=maximal_accuracy)
    _, later = entering((ends, local_grad), CTX, combine, identity, True)
    end_grad = jnp.sum(later * carried, axis=(1, 2))
    growth_grad = growth_grad.at[:, -1].add(end_grad)
    grads = backward((g_group, later, growth_grad))
    dx_list.append(grads[0])
    bmat_grad = grads[1]
    gram_grad = grads[2]
    dt_list.append(grads[3])
    rate_list.append(grads[4])
    bias_list.append(grads[5])
    skip_list.append(grads[6])
    cmat_grad = cmat_grad + jnp.dot(gram_grad, write_operator, precision=maximal_accuracy)
    bmat_grad = bmat_grad + jnp.dot(gram_grad.T, cmat, precision=maximal_accuracy)
    core = output_pieces[0].reshape(count, heads * width)
    channels_grad = dx_list[0]
    timestep_raw_gradient = dt_list[0]
    rate_grad = rate_list[0]
    bias_grad = bias_list[0]
    skip_grad = skip_list[0]
    shares = (
        summed_on_arrival(rate_grad, "dp", 0),
        summed_on_arrival(bias_grad, "dp", 0),
        summed_on_arrival(skip_grad, "dp", 0),
    )
    owned = packed_total((shares[0], shares[1], shares[2]), CTX)
    return (
        core.astype(jnp.bfloat16)[None],
        channels_grad.astype(jnp.bfloat16)[None],
        bmat_grad[None],
        cmat_grad[None],
        timestep_raw_gradient[None],
        owned[0],
        owned[1],
        owned[2],
    )


def solution(mesh):
    torus = Mesh(mesh.devices.reshape(mesh.shape["dp"], 4, 4, 2), ("dp", "ctx_0", "ctx_1", "ctx_2"))
    return jax.shard_map(
        local,
        mesh=torus,
        in_specs=(
            P("dp", CTX, None),
            P("dp", CTX, None),
            P("dp", CTX, None),
            P("dp", None, CTX),
            P("dp"),
            P("dp"),
            P("dp"),
            P("dp", CTX, None),
        ),
        out_specs=(
            P("dp", CTX, None),
            P("dp", CTX, None),
            P("dp", CTX, None),
            P("dp", CTX, None),
            P("dp", None, CTX),
            P("dp"),
            P("dp"),
            P("dp"),
        ),
        check_vma=False,
    )
```

profile of v0, /device:TPU:1, one launch (start us, length us, event | category | flops | bytes accessed | tf_op | source)
XLA Modules:
  0.0 376.4 jit_solution(17329192003138858828)
XLA Ops:
  7.9 20.4 %all-gather.4 = f32[8,8,3]{1,2,0:T(4,128)S(1)} all-gather(f32[1,8,3]{1,2,0:T(4,128)S(1)} %maximum_bitcast_fusion), channel_id=1, replica_groups=mesh['dp'=8,'ctx_0'=4,'ctx_1'=4,'ctx_2'=2] {'dp'}, dimensions={0}, use_global_device_ids=true | all-gather | bytes 864 | tf_op jit(solution)/shard_map/all_gather | solution.py:15
  34.4 1.6 fusion.71
  36.2 1.6 fusion.75
  40.8 8.6 %all-reduce.1 = f32[128]{0:T(128)S(1)} all-reduce(f32[128]{0:T(128)S(1)} %dynamic-update-slice.3), channel_id=2, replica_groups=mesh['dp'=8,'ctx_0'=4,'ctx_1'=4,'ctx_2'=2] {'ctx_2'}, use_global_device_ids=true, to_apply=%add.1 | all-reduce | flops 128 | bytes 1024
  49.5 7.6 %all-gather.24.cloned.1.call-done = f32[128,32,128]{2,1,0:T(8,128)} async-done(((f32[64,32,128]{2,1,0:T(8,128)}), f32[128,32,128]{2,1,0:T(8,128)}) %all-gather.24.cloned.1.call-update) | async-done | bytes 2097168 | tf_op jit(solution)/shard_map/all_gather | solution.py:36
  57.1 2.8 bitcast_add_fusion.16
  60.0 8.2 %all-reduce.2 = f32[256]{0:T(256)S(1)} all-reduce(f32[256]{0:T(256)S(1)} %get-tuple-element.107), channel_id=5, replica_groups=mesh['dp'=8,'ctx_0'=4,'ctx_1'=4,'ctx_2'=2] {'ctx_1'}, use_global_device_ids=true, to_apply=%add.2 | all-reduce | flops 256 | bytes 2048
  68.3 7.8 %all-gather.22.cloned.1.call-done = f32[128,32,128]{2,1,0:T(8,128)} async-done(((f32[64,32,128]{2,1,0:T(8,128)}), f32[128,32,128]{2,1,0:T(8,128)}) %all-gather.22.cloned.1.call-update) | async-done | bytes 2097168 | tf_op jit(solution)/shard_map/all_gather | solution.py:36
  76.1 2.7 bitcast_add_fusion.18
  78.9 50.5 %all-gather.18.cloned.1.call-done = f32[4,64,32,128]{3,2,1,0:T(8,128)} async-done(((f32[1,64,32,128]{3,2,1,0:T(8,128)}), f32[4,64,32,128]{3,2,1,0:T(8,128)}) %all-gather.18.cloned.1.call-update) | async-done | bytes 4194320 | tf_op jit(solution)/shard_map/all_gather | solution.py:36
  129.4 52.9 %all-gather.14.cloned.1.call-done = f32[4,64,32,128]{3,2,1,0:T(8,128)} async-done(((f32[1,64,32,128]{3,2,1,0:T(8,128)}), f32[4,64,32,128]{3,2,1,0:T(8,128)}) %all-gather.14.cloned.1.call-update) | async-done | bytes 4194320 | tf_op jit(solution)/shard_map/all_gather | solution.py:36
  182.3 4.8 %multiply_add_fusion = (f32[1,64,32,128]{3,2,1,0:T(8,128)}, f32[1,64,32,128]{3,2,1,0:T(8,128)}) fusion(f32[4,64,32,128]{3,2,1,0:T(8,128)} %all-gather.18.cloned.1.call-done, f32[64]{0:T(128)S(1)} %get-tuple-element.98, f32[64]{0:T(128)S(1)} %get-tuple-element.97, f32[64]{0:T(128)S(1)} %get-tuple-element.95, f32[64]{0:T(128)S(1)} %get-tuple-element.96, ...), kind=kLoop, calls=%fused_computation.86 | loop fusion | flops 3670016 | bytes 10487296 | tf_op jit(solution)/shard_map/add | solution.py:100
  188.5 6.7 %all-to-all-start.2 = ((f32[8,1,8]{2,1,0:T(1,128)}), f32[8,1,8]{2,1,0:T(1,128)S(1)}, u32[]{:S(2)}, u32[]{:S(2)}) async-start(f32[8,1,8]{2,1,0:T(1,128)} %bitcast.81), calls=%async_computation.2 | async-start | bytes 8192 | tf_op jit(solution)/shard_map/all_to_all | solution.py:54
  195.3 7.6 %all-gather.6 = f32[4,1,64]{2,1,0:T(1,128)S(1)} all-gather(f32[1,1,64]{2,1,0:T(1,128)S(1)} %get-tuple-element.92), channel_id=1, replica_groups=mesh['dp'=8,'ctx_0'=4,'ctx_1'=4,'ctx_2'=2] {'ctx_0'}, dimensions={0}, use_global_device_ids=true | all-gather | bytes 1280 | tf_op jit(solution)/shard_map/all_gather | solution.py:36
  202.9 6.2 %all-gather.5 = f32[4,1,64]{2,1,0:T(1,128)S(1)} all-gather(f32[1,1,64]{2,1,0:T(1,128)S(1)} %get-tuple-element.93), channel_id=1, replica_groups=mesh['dp'=8,'ctx_0'=4,'ctx_1'=4,'ctx_2'=2] {'ctx_0'}, dimensions={0}, use_global_device_ids=true | all-gather | bytes 1280 | tf_op jit(solution)/shard_map/all_gather | solution.py:36
  211.3 27.1 %all-gather.20.cloned.1.call-done = f32[4,64,32,128]{3,2,1,0:T(8,128)} async-done(((f32[1,64,32,128]{3,2,1,0:T(8,128)}), f32[4,64,32,128]{3,2,1,0:T(8,128)}) %all-gather.20.cloned.1.call-update) | async-done | bytes 4194320 | tf_op jit(solution)/shard_map/all_gather | solution.py:36
  238.4 5.0 %add_add_fusion = f32[1,64,32,128]{3,2,1,0:T(8,128)S(1)} fusion(f32[1,64,32,128]{3,2,1,0:T(8,128)} %get-tuple-element.100, f32[4,64,32,128]{3,2,1,0:T(8,128)} %all-gather.20.cloned.1.call-done, f32[4,64,32,128]{3,2,1,0:T(8,128)} %all-gather.18.cloned.1.call-done, f32[128,32,128]{2,1,0:T(8,128)} %all-gather.24.cloned.1.call-done, ...), kind=kLoop, calls=%fused_computation.85 | loop fusion | flops 7602176 | bytes 11537162 | tf_op jit(solution)/shard_map/add | solution.py:100
  244.4 1.9 convolution_bitcast_fusion.2
  246.3 45.0 %all-gather.16.cloned.1.call-done = f32[4,64,32,128]{3,2,1,0:T(8,128)} async-done(((f32[1,64,32,128]{3,2,1,0:T(8,128)}), f32[4,64,32,128]{3,2,1,0:T(8,128)}) %all-gather.16.cloned.1.call-update) | async-done | bytes 4194320 | tf_op jit(solution)/shard_map/all_gather | solution.py:36
  291.3 8.6 %fusion.50 = f32[64]{0:T(128)S(1)} fusion(f32[4,64,32,128]{3,2,1,0:T(8,128)} %all-gather.20.cloned.1.call-done, f32[4,64,32,128]{3,2,1,0:T(8,128)} %all-gather.18.cloned.1.call-done, f32[128,32,128]{2,1,0:T(8,128)} %all-gather.24.cloned.1.call-done, f32[4,64,32,128]{3,2,1,0:T(8,128)} %all-gather.16.cloned.1.call-done, ...), kind=kLoop, calls=%fused_computation.49 | loop fusion | flops 16777152 | bytes 20977428 | tf_op jit(solution)/shard_map/reduce_sum | solution.py:148
  300.0 3.0 fusion.43
  305.6 4.4 %add_add_fusion.1 = f32[1,64,32,128]{3,2,1,0:T(8,128)S(1)} fusion(f32[1,64,32,128]{3,2,1,0:T(8,128)} %get-tuple-element.101, f32[4,64,32,128]{3,2,1,0:T(8,128)} %all-gather.16.cloned.1.call-done, f32[4,64,32,128]{3,2,1,0:T(8,128)} %all-gather.14.cloned.1.call-done, f32[128,32,128]{2,1,0:T(8,128)S(1)} %copy-done.1, f32[64]{0:T(128)S(1)} %get-tuple-element.71, ...), kind=kLoop, calls=%fused_computation.89 | loop fusion | flops 7602176 | bytes 11537162 | tf_op jit(solution)/shard_map/add | solution.py:100
  311.0 1.7 fusion.59
  313.0 4.9 %fusion.7 = (f32[64,128]{1,0:T(8,128)S(1)}, f32[64,128]{1,0:T(8,128)S(1)}, f32[64,128]{1,0:T(8,128)S(1)}, f32[128,128]{1,0:T(8,128)S(1)}) fusion(f32[64,128]{1,0:T(8,128)} %get-tuple-element.76, f32[64,128]{1,0:T(8,128)S(1)} %reduce_window_sum.22, f32[128,128]{1,0:T(8,128)} %fusion.78, pred[128,128]{1,0:T(8,128)(4,1)} %iota_compare_fusion, ...), kind=kOutput, calls=%fused_computation.9 | convolution fusion | flops 80699392 | bytes 1359872 | tf_op jit(solution)/shard_map/transpose(jvp(hts,shp->thp))/dot_general | solution.py:91
  320.8 6.7 %all-to-all-start.1 = ((f32[8,1,8]{2,1,0:T(1,128)}), f32[8,1,8]{2,1,0:T(1,128)S(1)}, u32[]{:S(2)}, u32[]{:S(2)}) async-start(f32[8,1,8]{2,1,0:T(1,128)} %bitcast.80), calls=%async_computation.1 | async-start | bytes 8192 | tf_op jit(solution)/shard_map/all_to_all | solution.py:54
  327.6 5.7 %fusion.38 = bf16[128,64,32]{0,2,1:T(8,128)(2,1)S(1)} fusion(bf16[128,64,32]{0,2,1:T(8,128)(2,1)S(1)} %bitcast.326, f32[64,128]{1,0:T(8,128)} %get-tuple-element.76, f32[64,128]{1,0:T(8,128)S(1)} %reduce_window_sum.22, f32[128,128]{1,0:T(8,128)} %fusion.78, pred[128,128]{1,0:T(8,128)(4,1)} %iota_compare_fusion, f32[64,32,128]{2,1,0:T(8,128)} %get-tuple-element.113, ...), kind=kOutput, calls=%fused_computation.34 | convolution fusion | flops 408420352 | bytes 2277632 | tf_op jit(solution)/shard_map/jvp(hts,shp->thp)/dot_general | solution.py:91
  333.4 3.5 fusion.35
  337.0 1.8 convolution_bitcast_fusion.1
  339.5 6.6 %all-to-all-start = ((f32[8,1,8]{2,1,0:T(1,128)}), f32[8,1,8]{2,1,0:T(1,128)S(1)}, u32[]{:S(2)}, u32[]{:S(2)}) async-start(f32[8,1,8]{2,1,0:T(1,128)} %bitcast.79), calls=%async_computation | async-start | bytes 8192 | tf_op jit(solution)/shard_map/all_to_all | solution.py:54
  347.0 5.6 %all-to-all-done = f32[8,1,8]{2,1,0:T(1,128)S(1)} async-done(((f32[8,1,8]{2,1,0:T(1,128)}), f32[8,1,8]{2,1,0:T(1,128)S(1)}, u32[]{:S(2)}, u32[]{:S(2)}) %all-to-all-start) | async-done | bytes 288 | tf_op jit(solution)/shard_map/all_to_all | solution.py:54
  353.3 8.6 %all-to-all-start.3 = ((f32[32,1,24]{2,1,0:T(1,128)}), f32[32,1,24]{2,1,0:T(1,128)S(1)}, u32[]{:S(2)}, u32[]{:S(2)}) async-start(f32[32,1,24]{2,1,0:T(1,128)} %broadcast_in_dim.71), calls=%async_computation.3 | async-start | bytes 32768 | tf_op jit(solution)/shard_map/all_to_all | solution.py:60
  364.8 4.0 %all-to-all-done.3 = f32[32,1,24]{2,1,0:T(1,128)S(1)} async-done(((f32[32,1,24]{2,1,0:T(1,128)}), f32[32,1,24]{2,1,0:T(1,128)S(1)}, u32[]{:S(2)}, u32[]{:S(2)}) %all-to-all-start.3) | async-done | bytes 3104 | tf_op jit(solution)/shard_map/all_to_all | solution.py:60
  (118 shorter events, 26.3 us)
Async XLA Ops:
  7.2 29.0 %copy-start = (bf16[1,128,128]{2,1,0:T(8,128)(2,1)S(1)}, bf16[1,128,128]{2,1,0:T(8,128)(2,1)}, u32[]{:S(2)}) copy-start(bf16[1,128,128]{2,1,0:T(8,128)(2,1)} %param.11) | copy-start | bytes 98308
  7.2 27.3 %copy-start.13 = (bf16[1,128,128]{2,1,0:T(8,128)(2,1)S(1)}, bf16[1,128,128]{2,1,0:T(8,128)(2,1)}, u32[]{:S(2)}) copy-start(bf16[1,128,128]{2,1,0:T(8,128)(2,1)} %param.12) | copy-start | bytes 98308
  7.2 49.9 %all-gather.24.cloned.1.call-start = ((), (), s32[]{:S(2)}) async-start(), calls=%async_computation.9 | async-start | bytes 3145728 | tf_op jit(solution)/shard_map/all_gather | solution.py:36
  32.5 5.3 %copy-start.7 = (bf16[1,128,2048]{1,2,0:T(8,128)(2,1)}, bf16[1,128,2048]{1,2,0:T(8,128)(2,1)S(1)}, u32[]{:S(2)}) copy-start(bf16[1,128,2048]{1,2,0:T(8,128)(2,1)S(1)} %copy.70) | copy-start | bytes 1572868
  34.0 3.8 %copy-start.25 = (u32[256]{0:T(256)S(1)}, u32[256]{0:T(256)}, u32[]{:S(2)}) copy-start(u32[256]{0:T(256)} %constant.82) | copy-start | bytes 3076
  34.1 4.4 %copy-start.24 = (u32[256]{0:T(256)S(1)}, u32[256]{0:T(256)}, u32[]{:S(2)}) copy-start(u32[256]{0:T(256)} %constant.77) | copy-start | bytes 3076
  34.4 25.5 %copy-start.2 = (f32[1,128,2048]{1,2,0:T(8,128)}, f32[1,128,2048]{1,2,0:T(8,128)S(1)}, u32[]{:S(2)}) copy-start(f32[1,128,2048]{1,2,0:T(8,128)S(1)} %get-tuple-element.74) | copy-start | bytes 3145732
  36.1 40.0 %all-gather.22.cloned.1.call-start = ((), (), s32[]{:S(2)}) async-start(), calls=%async_computation.8 | async-start | bytes 3145728 | tf_op jit(solution)/shard_map/all_gather | solution.py:36
  37.8 91.6 %all-gather.18.cloned.1.call-start = ((), (), s32[]{:S(2)}) async-start(), calls=%async_computation.6 | async-start | bytes 5242880 | tf_op jit(solution)/shard_map/all_gather | solution.py:36
  59.9 122.4 %all-gather.14.cloned.1.call-start = ((), (), s32[]{:S(2)}) async-start(), calls=%async_computation.4 | async-start | bytes 5242880 | tf_op jit(solution)/shard_map/all_gather | solution.py:36
  78.9 159.5 %all-gather.20.cloned.1.call-start = ((), (), s32[]{:S(2)}) async-start(), calls=%async_computation.7 | async-start | bytes 5242880 | tf_op jit(solution)/shard_map/all_gather | solution.py:36
  187.1 104.2 %all-gather.16.cloned.1.call-start = ((), (), s32[]{:S(2)}) async-start(), calls=%async_computation.5 | async-start | bytes 5242880 | tf_op jit(solution)/shard_map/all_gather | solution.py:36
  188.5 22.1 %all-to-all-start.2 = ((f32[8,1,8]{2,1,0:T(1,128)}), f32[8,1,8]{2,1,0:T(1,128)S(1)}, u32[]{:S(2)}, u32[]{:S(2)}) async-start(f32[8,1,8]{2,1,0:T(1,128)} %bitcast.81), calls=%async_computation.2 | async-start | bytes 8192 | tf_op jit(solution)/shard_map/all_to_all | solution.py:54
  209.7 81.6 %copy-start.19 = (f32[64]{0:T(128)}, f32[64]{0:T(128)S(1)}, u32[]{:S(2)}) copy-start(f32[64]{0:T(128)S(1)} %get-tuple-element.89) | copy-start | bytes 772
  209.7 81.6 %copy-start.20 = (f32[64]{0:T(128)}, f32[64]{0:T(128)S(1)}, u32[]{:S(2)}) copy-start(f32[64]{0:T(128)S(1)} %get-tuple-element.90) | copy-start | bytes 772
  209.7 81.6 %copy-start.21 = (f32[64]{0:T(128)}, f32[64]{0:T(128)S(1)}, u32[]{:S(2)}) copy-start(f32[64]{0:T(128)S(1)} %get-tuple-element.91) | copy-start | bytes 772
  238.4 6.0 %copy-start.3 = (f32[1,128,2048]{1,2,0:T(8,128)S(1)}, f32[1,128,2048]{1,2,0:T(8,128)}, u32[]{:S(2)}) copy-start(f32[1,128,2048]{1,2,0:T(8,128)} %copy-done.2) | copy-start | bytes 3145732
  238.4 52.9 %copy-start.1 = (f32[128,32,128]{2,1,0:T(8,128)S(1)}, f32[128,32,128]{2,1,0:T(8,128)}, u32[]{:S(2)}) copy-start(f32[128,32,128]{2,1,0:T(8,128)} %all-gather.22.cloned.1.call-done) | copy-start | bytes 6291460
  291.3 11.7 %copy-start.14 = (f32[1,64,128]{2,1,0:T(8,128)S(1)}, f32[1,64,128]{2,1,0:T(8,128)}, u32[]{:S(2)}) copy-start(f32[1,64,128]{2,1,0:T(8,128)} %param.13) | copy-start | bytes 98308
  305.6 5.4 %copy-start.8 = (bf16[1,128,2048]{1,2,0:T(8,128)(2,1)S(1)}, bf16[1,128,2048]{1,2,0:T(8,128)(2,1)}, u32[]{:S(2)}) copy-start(bf16[1,128,2048]{1,2,0:T(8,128)(2,1)} %copy-done.7) | copy-start | bytes 1572868
  313.0 4.9 %copy-start.15 = (f32[64,1]{1,0:T(8,128)S(1)}, f32[64,1]{1,0:T(8,128)}, u32[]{:S(2)}) copy-start(f32[64,1]{1,0:T(8,128)} %copy.73) | copy-start | bytes 772
  313.0 14.5 %copy-start.11 = (bf16[1,128,2048]{1,2,0:T(8,128)(2,1)S(1)}, bf16[1,128,2048]{1,2,0:T(8,128)(2,1)}, u32[]{:S(2)}) copy-start(bf16[1,128,2048]{1,2,0:T(8,128)(2,1)} %copy-done.10) | copy-start | bytes 1572868
  320.8 18.7 %all-to-all-start.1 = ((f32[8,1,8]{2,1,0:T(1,128)}), f32[8,1,8]{2,1,0:T(1,128)S(1)}, u32[]{:S(2)}, u32[]{:S(2)}) async-start(f32[8,1,8]{2,1,0:T(1,128)} %bitcast.80), calls=%async_computation.1 | async-start | bytes 8192 | tf_op jit(solution)/shard_map/all_to_all | solution.py:54
  327.5 5.8 %copy-start.9 = (bf16[1,128,2048]{1,2,0:T(8,128)(2,1)S(1)}, bf16[1,128,2048]{1,2,0:T(8,128)(2,1)}, u32[]{:S(2)}) copy-start(bf16[1,128,2048]{1,2,0:T(8,128)(2,1)} %copy-done.7) | copy-start | bytes 1572868
  327.5 5.8 %copy-start.12 = (f32[128,64,32]{0,2,1:T(8,128)S(1)}, f32[128,64,32]{0,2,1:T(8,128)}, u32[]{:S(2)}) copy-start(f32[128,64,32]{0,2,1:T(8,128)} %get-tuple-element.111) | copy-start | bytes 3145732
  327.5 5.8 %copy-start.16 = (f32[128,128]{1,0:T(8,128)S(1)}, f32[128,128]{1,0:T(8,128)}, u32[]{:S(2)}) copy-start(f32[128,128]{1,0:T(8,128)} %fusion.78) | copy-start | bytes 196612
  327.6 5.8 %copy-start.17 = (f32[64,128]{1,0:T(8,128)S(1)}, f32[64,128]{1,0:T(8,128)}, u32[]{:S(2)}) copy-start(f32[64,128]{1,0:T(8,128)} %get-tuple-element.76) | copy-start | bytes 98308
  327.6 5.8 %copy-start.18 = (pred[128,128]{1,0:T(8,128)(4,1)S(1)}, pred[128,128]{1,0:T(8,128)(4,1)}, u32[]{:S(2)}) copy-start(pred[128,128]{1,0:T(8,128)(4,1)} %iota_compare_fusion) | copy-start | bytes 49156
  327.6 5.8 %copy-start.23 = (f32[64]{0:T(128)S(1)}, f32[64]{0:T(128)}, u32[]{:S(2)}) copy-start(f32[64]{0:T(128)} %get-tuple-element.81) | copy-start | bytes 772
  333.4 19.2 %copy-start.22 = (f32[8]{0:T(128)S(1)}, f32[8]{0:T(128)}, u32[]{:S(2)}) copy-start(f32[8]{0:T(128)} %reduce_sum.179) | copy-start | bytes 100
  339.5 13.1 %all-to-all-start = ((f32[8,1,8]{2,1,0:T(1,128)}), f32[8,1,8]{2,1,0:T(1,128)S(1)}, u32[]{:S(2)}, u32[]{:S(2)}) async-start(f32[8,1,8]{2,1,0:T(1,128)} %bitcast.79), calls=%async_computation | async-start | bytes 8192 | tf_op jit(solution)/shard_map/all_to_all | solution.py:54
  353.3 15.6 %all-to-all-start.3 = ((f32[32,1,24]{2,1,0:T(1,128)}), f32[32,1,24]{2,1,0:T(1,128)S(1)}, u32[]{:S(2)}, u32[]{:S(2)}) async-start(f32[32,1,24]{2,1,0:T(1,128)} %broadcast_in_dim.71), calls=%async_computation.3 | async-start | bytes 32768 | tf_op jit(solution)/shard_map/all_to_all | solution.py:60
  (4 other events, 9.3 us)
Sparse Core Ops, SparseCore 0:
  36.2 20.8 all-gather.23
  58.9 17.1 all-gather.21
  77.9 51.4 all-gather.17
  131.1 51.1 all-gather.13
  187.2 51.1 all-gather.19
  240.1 51.1 all-gather.15
where the time goes:
time: 377 us; the launch traced here: 376 us
  waiting for transfers between devices  201 us (53%)
  blocking collectives  50.9 us (14%)
  other arithmetic  37.9 us (10%)
  starting transfers between devices  29 us (8%)
  matrix products  28.2 us (7%)
  between operations  15.9 us (4%)
  local copies, waits for them, and re-layouts  13.2 us (4%)
    all_gather x6, waiting for transfers between devices, entering(): pieces = jax.tree.map(lambda part: lax.all_gather(part, axis), subtotal)  191 us
    all_gather x1, blocking collectives, rows_first(): result = lax.all_gather(both, axis, axis=0, tiled=True)  20.4 us
    all_to_all x3, starting transfers between devices, summed_on_arrival(): lax.all_to_all(split_up(array, dim, devices), axis, 0, 0, tiled=True)  20.1 us
    add x5, other arithmetic, combine(): later[0][:, None, None] * earlier[1] + later[1]  19.6 us
    unnamed x2, blocking collectives  16.7 us
    dot_general x3, matrix products, local_part(): inner = jnp.einsum('hts,shp->thp', weights, xg3, precision=maximal_accuracy)  14.2 us
    all_gather x2, blocking collectives, entering(): pieces = jax.tree.map(lambda part: lax.all_gather(part, axis), subtotal)  13.7 us
    all_to_all x1, starting transfers between devices, copy_for_each(): lax.all_to_all(jnp.broadcast_to(array[None], (devices, *array.shape)), ax...  8.61 us
  transfers between devices with their start and end apart: 10, of which 8 were waited for; matrix products, arithmetic and copies ran while one was open for 9% of the time, Pallas kernels for 0%

commit v1 on v0

--- a/solution.py
+++ b/solution.py
@@ -12,7 +12,9 @@
     turned = [jnp.moveaxis(a, dim, 0) for a, dim in zip(arrays, dims)]
     widths = [t[0].size for t in turned]
     both = jnp.concatenate([t.reshape(-1, w) for t, w in zip(turned, widths)], axis=1)
-    result = lax.all_gather(both, axis, axis=0, tiled=True)
+    result = jnp.concatenate(
+        lax.all_to_all(jnp.stack([both] * lax.axis_size(axis)), axis, 0, 0), axis=0
+    )
     tiles = jnp.split(result, [sum(widths[:k]) for k in range(1, len(widths))], axis=1)
     return tuple(
         (

time: 377 us -> 364 us (0.966)
  blocking collectives: 50.9 us -> 26.1 us
  starting transfers between devices: 29 us -> 38 us
    all_gather x1 -> x0, blocking collectives: 20.4 us -> none  [rows_first(): result = lax.all_gather(both, axis, axis=0, tiled=True)]
    all_to_all x0 -> x1, starting transfers between devices: none -> 9.01 us  [rows_first(): lax.all_to_all(jnp.stack([both] * lax.axis_size(axis)), axis, 0, 0)]
    unnamed x2, blocking collectives: 16.7 us -> 12.4 us
    unnamed x62 -> x61, local copies, waits for them, and re-layouts: 8.43 us -> 8.32 us
  transfers between devices with their start and end apart: 10 -> 11, of which waited for: 8 -> 9; matrix products, arithmetic and copies ran while one was open for 9% -> 10% of each run, Pallas kernels for 0% -> 0%
where the time goes in v1:
time: 364 us; the launch traced here: 363 us
  waiting for transfers between devices  203 us (56%)
  starting transfers between devices  38 us (10%)
  other arithmetic  37.8 us (10%)
  matrix products  28.2 us (8%)
  blocking collectives  26.1 us (7%)
  between operations  15.9 us (4%)
  local copies, waits for them, and re-layouts  13.8 us (4%)
    all_gather x6, waiting for transfers between devices, entering(): pieces = jax.tree.map(lambda part: lax.all_gather(part, axis), subtotal)  189 us
    all_to_all x3, starting transfers between devices, summed_on_arrival(): lax.all_to_all(split_up(array, dim, devices), axis, 0, 0, tiled=True)  20.1 us
    add x5, other arithmetic, combine(): later[0][:, None, None] * earlier[1] + later[1]  19.6 us
    dot_general x3, matrix products, local_part(): inner = jnp.einsum('hts,shp->thp', weights, xg3, precision=maximal_accuracy)  14.2 us
    all_gather x2, blocking collectives, entering(): pieces = jax.tree.map(lambda part: lax.all_gather(part, axis), subtotal)  13.7 us
    unnamed x2, blocking collectives  12.4 us
    all_to_all x1, starting transfers between devices, rows_first(): lax.all_to_all(jnp.stack([both] * lax.axis_size(axis)), axis, 0, 0)  9.01 us
    all_to_all x1, starting transfers between devices, copy_for_each(): lax.all_to_all(jnp.broadcast_to(array[None], (devices, *array.shape)), ax...  8.61 us
  transfers between devices with their start and end apart: 11, of which 9 were waited for; matrix products, arithmetic and copies ran while one was open for 10% of the time, Pallas kernels for 0%

profile of v1, /device:TPU:1, one launch (start us, length us, event | category | flops | bytes accessed | tf_op | source)
XLA Modules:
  0.0 363.3 jit_solution(9746469955427785559)
XLA Ops:
  8.5 9.0 %all-to-all-start = ((f32[8,8,3]{1,2,0:T(4,128)}), f32[8,8,3]{1,2,0:T(4,128)S(1)}, u32[]{:S(2)}, u32[]{:S(2)}) async-start(f32[8,8,3]{1,2,0:T(4,128)} %stack.2), calls=%async_computation | async-start | bytes 32768 | tf_op jit(solution)/shard_map/all_to_all | solution.py:16
  20.4 3.7 %all-to-all-done = f32[8,8,3]{1,2,0:T(4,128)S(1)} async-done(((f32[8,8,3]{1,2,0:T(4,128)}), f32[8,8,3]{1,2,0:T(4,128)S(1)}, u32[]{:S(2)}, u32[]{:S(2)}) %all-to-all-start) | async-done | bytes 800 | tf_op jit(solution)/shard_map/all_to_all | solution.py:16
  27.4 1.6 fusion.71
  33.7 4.2 %all-reduce.1 = f32[128]{0:T(128)S(1)} all-reduce(f32[128]{0:T(128)S(1)} %dynamic-update-slice.3), channel_id=2, replica_groups=mesh['dp'=8,'ctx_0'=4,'ctx_1'=4,'ctx_2'=2] {'ctx_2'}, use_global_device_ids=true, to_apply=%add.1 | all-reduce | flops 128 | bytes 1024
  38.0 6.1 %all-gather.23.cloned.1.call-done = f32[128,32,128]{2,1,0:T(8,128)} async-done(((f32[64,32,128]{2,1,0:T(8,128)}), f32[128,32,128]{2,1,0:T(8,128)}) %all-gather.23.cloned.1.call-update) | async-done | bytes 2097168 | tf_op jit(solution)/shard_map/all_gather | solution.py:38
  44.1 2.8 bitcast_add_fusion.16
  47.0 8.2 %all-reduce.2 = f32[256]{0:T(256)S(1)} all-reduce(f32[256]{0:T(256)S(1)} %get-tuple-element.115), channel_id=5, replica_groups=mesh['dp'=8,'ctx_0'=4,'ctx_1'=4,'ctx_2'=2] {'ctx_1'}, use_global_device_ids=true, to_apply=%add.2 | all-reduce | flops 256 | bytes 2048
  55.3 7.9 %all-gather.21.cloned.1.call-done = f32[128,32,128]{2,1,0:T(8,128)} async-done(((f32[64,32,128]{2,1,0:T(8,128)}), f32[128,32,128]{2,1,0:T(8,128)}) %all-gather.21.cloned.1.call-update) | async-done | bytes 2097168 | tf_op jit(solution)/shard_map/all_gather | solution.py:38
  63.1 2.7 bitcast_add_fusion.18
  65.9 50.5 %all-gather.17.cloned.1.call-done = f32[4,64,32,128]{3,2,1,0:T(8,128)} async-done(((f32[1,64,32,128]{3,2,1,0:T(8,128)}), f32[4,64,32,128]{3,2,1,0:T(8,128)}) %all-gather.17.cloned.1.call-update) | async-done | bytes 4194320 | tf_op jit(solution)/shard_map/all_gather | solution.py:38
  116.4 52.9 %all-gather.13.cloned.1.call-done = f32[4,64,32,128]{3,2,1,0:T(8,128)} async-done(((f32[1,64,32,128]{3,2,1,0:T(8,128)}), f32[4,64,32,128]{3,2,1,0:T(8,128)}) %all-gather.13.cloned.1.call-update) | async-done | bytes 4194320 | tf_op jit(solution)/shard_map/all_gather | solution.py:38
  169.3 4.7 %multiply_add_fusion = (f32[1,64,32,128]{3,2,1,0:T(8,128)}, f32[1,64,32,128]{3,2,1,0:T(8,128)}) fusion(f32[4,64,32,128]{3,2,1,0:T(8,128)} %all-gather.17.cloned.1.call-done, f32[64]{0:T(128)S(1)} %get-tuple-element.106, f32[64]{0:T(128)S(1)} %get-tuple-element.105, f32[64]{0:T(128)S(1)} %get-tuple-element.103, f32[64]{0:T(128)S(1)} %get-tuple-element.104, ...), kind=kLoop, calls=%fused_computation.86 | loop fusion | flops 3670016 | bytes 10487296 | tf_op jit(solution)/shard_map/add | solution.py:102
  176.9 6.7 %all-to-all-start.3 = ((f32[8,1,8]{2,1,0:T(1,128)}), f32[8,1,8]{2,1,0:T(1,128)S(1)}, u32[]{:S(2)}, u32[]{:S(2)}) async-start(f32[8,1,8]{2,1,0:T(1,128)} %bitcast.80), calls=%async_computation.3 | async-start | bytes 8192 | tf_op jit(solution)/shard_map/all_to_all | solution.py:56
  183.7 7.6 %all-gather.5 = f32[4,1,64]{2,1,0:T(1,128)S(1)} all-gather(f32[1,1,64]{2,1,0:T(1,128)S(1)} %get-tuple-element.100), channel_id=1, replica_groups=mesh['dp'=8,'ctx_0'=4,'ctx_1'=4,'ctx_2'=2] {'ctx_0'}, dimensions={0}, use_global_device_ids=true | all-gather | bytes 1280 | tf_op jit(solution)/shard_map/all_gather | solution.py:38
  191.3 6.2 %all-gather.4 = f32[4,1,64]{2,1,0:T(1,128)S(1)} all-gather(f32[1,1,64]{2,1,0:T(1,128)S(1)} %get-tuple-element.101), channel_id=1, replica_groups=mesh['dp'=8,'ctx_0'=4,'ctx_1'=4,'ctx_2'=2] {'ctx_0'}, dimensions={0}, use_global_device_ids=true | all-gather | bytes 1280 | tf_op jit(solution)/shard_map/all_gather | solution.py:38
  198.2 27.2 %all-gather.19.cloned.1.call-done = f32[4,64,32,128]{3,2,1,0:T(8,128)} async-done(((f32[1,64,32,128]{3,2,1,0:T(8,128)}), f32[4,64,32,128]{3,2,1,0:T(8,128)}) %all-gather.19.cloned.1.call-update) | async-done | bytes 4194320 | tf_op jit(solution)/shard_map/all_gather | solution.py:38
  225.4 5.0 %add_add_fusion = f32[1,64,32,128]{3,2,1,0:T(8,128)S(1)} fusion(f32[1,64,32,128]{3,2,1,0:T(8,128)} %get-tuple-element.108, f32[4,64,32,128]{3,2,1,0:T(8,128)} %all-gather.19.cloned.1.call-done, f32[4,64,32,128]{3,2,1,0:T(8,128)} %all-gather.17.cloned.1.call-done, f32[128,32,128]{2,1,0:T(8,128)} %all-gather.23.cloned.1.call-done, ...), kind=kLoop, calls=%fused_computation.85 | loop fusion | flops 7602176 | bytes 11537162 | tf_op jit(solution)/shard_map/add | solution.py:102
  231.4 1.9 convolution_bitcast_fusion.2
  233.2 45.0 %all-gather.15.cloned.1.call-done = f32[4,64,32,128]{3,2,1,0:T(8,128)} async-done(((f32[1,64,32,128]{3,2,1,0:T(8,128)}), f32[4,64,32,128]{3,2,1,0:T(8,128)}) %all-gather.15.cloned.1.call-update) | async-done | bytes 4194320 | tf_op jit(solution)/shard_map/all_gather | solution.py:38
  278.3 8.6 %fusion.50 = f32[64]{0:T(128)S(1)} fusion(f32[4,64,32,128]{3,2,1,0:T(8,128)} %all-gather.19.cloned.1.call-done, f32[4,64,32,128]{3,2,1,0:T(8,128)} %all-gather.17.cloned.1.call-done, f32[128,32,128]{2,1,0:T(8,128)} %all-gather.23.cloned.1.call-done, f32[4,64,32,128]{3,2,1,0:T(8,128)} %all-gather.15.cloned.1.call-done, ...), kind=kLoop, calls=%fused_computation.49 | loop fusion | flops 16777152 | bytes 20977428 | tf_op jit(solution)/shard_map/reduce_sum | solution.py:150
  287.0 3.0 fusion.43
  292.6 4.4 %add_add_fusion.1 = f32[1,64,32,128]{3,2,1,0:T(8,128)S(1)} fusion(f32[1,64,32,128]{3,2,1,0:T(8,128)} %get-tuple-element.109, f32[4,64,32,128]{3,2,1,0:T(8,128)} %all-gather.15.cloned.1.call-done, f32[4,64,32,128]{3,2,1,0:T(8,128)} %all-gather.13.cloned.1.call-done, f32[128,32,128]{2,1,0:T(8,128)S(1)} %copy-done.1, f32[64]{0:T(128)S(1)} %get-tuple-element.79, ...), kind=kLoop, calls=%fused_computation.89 | loop fusion | flops 7602176 | bytes 11537162 | tf_op jit(solution)/shard_map/add | solution.py:102
  298.0 1.7 fusion.59
  300.0 4.9 %fusion.7 = (f32[64,128]{1,0:T(8,128)S(1)}, f32[64,128]{1,0:T(8,128)S(1)}, f32[64,128]{1,0:T(8,128)S(1)}, f32[128,128]{1,0:T(8,128)S(1)}) fusion(f32[64,128]{1,0:T(8,128)} %get-tuple-element.84, f32[64,128]{1,0:T(8,128)S(1)} %reduce_window_sum.22, f32[128,128]{1,0:T(8,128)} %fusion.78, pred[128,128]{1,0:T(8,128)(4,1)} %iota_compare_fusion, ...), kind=kOutput, calls=%fused_computation.9 | convolution fusion | flops 80699392 | bytes 1359872 | tf_op jit(solution)/shard_map/transpose(jvp(hts,shp->thp))/dot_general | solution.py:93
  307.7 6.7 %all-to-all-start.2 = ((f32[8,1,8]{2,1,0:T(1,128)}), f32[8,1,8]{2,1,0:T(1,128)S(1)}, u32[]{:S(2)}, u32[]{:S(2)}) async-start(f32[8,1,8]{2,1,0:T(1,128)} %bitcast.79), calls=%async_computation.2 | async-start | bytes 8192 | tf_op jit(solution)/shard_map/all_to_all | solution.py:56
  314.5 5.7 %fusion.38 = bf16[128,64,32]{0,2,1:T(8,128)(2,1)S(1)} fusion(bf16[128,64,32]{0,2,1:T(8,128)(2,1)S(1)} %bitcast.324, f32[64,128]{1,0:T(8,128)} %get-tuple-element.84, f32[64,128]{1,0:T(8,128)S(1)} %reduce_window_sum.22, f32[128,128]{1,0:T(8,128)} %fusion.78, pred[128,128]{1,0:T(8,128)(4,1)} %iota_compare_fusion, f32[64,32,128]{2,1,0:T(8,128)} %get-tuple-element.121, ...), kind=kOutput, calls=%fused_computation.34 | convolution fusion | flops 408420352 | bytes 2277632 | tf_op jit(solution)/shard_map/jvp(hts,shp->thp)/dot_general | solution.py:93
  320.4 3.5 fusion.35
  323.9 1.8 convolution_bitcast_fusion.1
  326.4 6.6 %all-to-all-start.1 = ((f32[8,1,8]{2,1,0:T(1,128)}), f32[8,1,8]{2,1,0:T(1,128)S(1)}, u32[]{:S(2)}, u32[]{:S(2)}) async-start(f32[8,1,8]{2,1,0:T(1,128)} %bitcast.78), calls=%async_computation.1 | async-start | bytes 8192 | tf_op jit(solution)/shard_map/all_to_all | solution.py:56
  333.9 5.6 %all-to-all-done.1 = f32[8,1,8]{2,1,0:T(1,128)S(1)} async-done(((f32[8,1,8]{2,1,0:T(1,128)}), f32[8,1,8]{2,1,0:T(1,128)S(1)}, u32[]{:S(2)}, u32[]{:S(2)}) %all-to-all-start.1) | async-done | bytes 288 | tf_op jit(solution)/shard_map/all_to_all | solution.py:56
  340.3 8.6 %all-to-all-start.4 = ((f32[32,1,24]{2,1,0:T(1,128)}), f32[32,1,24]{2,1,0:T(1,128)S(1)}, u32[]{:S(2)}, u32[]{:S(2)}) async-start(f32[32,1,24]{2,1,0:T(1,128)} %broadcast_in_dim.71), calls=%async_computation.4 | async-start | bytes 32768 | tf_op jit(solution)/shard_map/all_to_all | solution.py:62
  351.8 4.0 %all-to-all-done.4 = f32[32,1,24]{2,1,0:T(1,128)S(1)} async-done(((f32[32,1,24]{2,1,0:T(1,128)}), f32[32,1,24]{2,1,0:T(1,128)S(1)}, u32[]{:S(2)}, u32[]{:S(2)}) %all-to-all-start.4) | async-done | bytes 3104 | tf_op jit(solution)/shard_map/all_to_all | solution.py:62
  (120 shorter events, 28.4 us)
Async XLA Ops:
  7.2 21.9 %copy-start = (bf16[1,128,128]{2,1,0:T(8,128)(2,1)S(1)}, bf16[1,128,128]{2,1,0:T(8,128)(2,1)}, u32[]{:S(2)}) copy-start(bf16[1,128,128]{2,1,0:T(8,128)(2,1)} %param.11) | copy-start | bytes 98308
  7.2 20.2 %copy-start.13 = (bf16[1,128,128]{2,1,0:T(8,128)(2,1)S(1)}, bf16[1,128,128]{2,1,0:T(8,128)(2,1)}, u32[]{:S(2)}) copy-start(bf16[1,128,128]{2,1,0:T(8,128)(2,1)} %param.12) | copy-start | bytes 98308
  8.5 15.6 %all-to-all-start = ((f32[8,8,3]{1,2,0:T(4,128)}), f32[8,8,3]{1,2,0:T(4,128)S(1)}, u32[]{:S(2)}, u32[]{:S(2)}) async-start(f32[8,8,3]{1,2,0:T(4,128)} %stack.2), calls=%async_computation | async-start | bytes 32768 | tf_op jit(solution)/shard_map/all_to_all | solution.py:16
  17.5 26.6 %all-gather.23.cloned.1.call-start = ((), (), s32[]{:S(2)}) async-start(), calls=%async_computation.10 | async-start | bytes 3145728 | tf_op jit(solution)/shard_map/all_gather | solution.py:38
  18.9 11.8 %copy-start.7 = (bf16[1,128,2048]{1,2,0:T(8,128)(2,1)}, bf16[1,128,2048]{1,2,0:T(8,128)(2,1)S(1)}, u32[]{:S(2)}) copy-start(bf16[1,128,2048]{1,2,0:T(8,128)(2,1)S(1)} %copy.80) | copy-start | bytes 1572868
  20.4 10.3 %copy-start.10 = (bf16[1,128,2048]{1,2,0:T(8,128)(2,1)}, bf16[1,128,2048]{1,2,0:T(8,128)(2,1)S(1)}, u32[]{:S(2)}) copy-start(bf16[1,128,2048]{1,2,0:T(8,128)(2,1)S(1)} %copy.78) | copy-start | bytes 1572868
  27.3 19.6 %copy-start.2 = (f32[1,128,2048]{1,2,0:T(8,128)}, f32[1,128,2048]{1,2,0:T(8,128)S(1)}, u32[]{:S(2)}) copy-start(f32[1,128,2048]{1,2,0:T(8,128)S(1)} %get-tuple-element.82) | copy-start | bytes 3145732
  29.0 34.1 %all-gather.21.cloned.1.call-start = ((), (), s32[]{:S(2)}) async-start(), calls=%async_computation.9 | async-start | bytes 3145728 | tf_op jit(solution)/shard_map/all_gather | solution.py:38
  30.7 85.7 %all-gather.17.cloned.1.call-start = ((), (), s32[]{:S(2)}) async-start(), calls=%async_computation.7 | async-start | bytes 5242880 | tf_op jit(solution)/shard_map/all_gather | solution.py:38
  46.9 122.4 %all-gather.13.cloned.1.call-start = ((), (), s32[]{:S(2)}) async-start(), calls=%async_computation.5 | async-start | bytes 5242880 | tf_op jit(solution)/shard_map/all_gather | solution.py:38
  65.9 159.5 %all-gather.19.cloned.1.call-start = ((), (), s32[]{:S(2)}) async-start(), calls=%async_computation.8 | async-start | bytes 5242880 | tf_op jit(solution)/shard_map/all_gather | solution.py:38
  174.1 104.2 %all-gather.15.cloned.1.call-start = ((), (), s32[]{:S(2)}) async-start(), calls=%async_computation.6 | async-start | bytes 5242880 | tf_op jit(solution)/shard_map/all_gather | solution.py:38
  176.9 20.7 %all-to-all-start.3 = ((f32[8,1,8]{2,1,0:T(1,128)}), f32[8,1,8]{2,1,0:T(1,128)S(1)}, u32[]{:S(2)}, u32[]{:S(2)}) async-start(f32[8,1,8]{2,1,0:T(1,128)} %bitcast.80), calls=%async_computation.3 | async-start | bytes 8192 | tf_op jit(solution)/shard_map/all_to_all | solution.py:56
  197.5 80.8 %copy-start.19 = (f32[64]{0:T(128)}, f32[64]{0:T(128)S(1)}, u32[]{:S(2)}) copy-start(f32[64]{0:T(128)S(1)} %get-tuple-element.97) | copy-start | bytes 772
  197.5 80.8 %copy-start.20 = (f32[64]{0:T(128)}, f32[64]{0:T(128)S(1)}, u32[]{:S(2)}) copy-start(f32[64]{0:T(128)S(1)} %get-tuple-element.98) | copy-start | bytes 772
  197.5 80.7 %copy-start.21 = (f32[64]{0:T(128)}, f32[64]{0:T(128)S(1)}, u32[]{:S(2)}) copy-start(f32[64]{0:T(128)S(1)} %get-tuple-element.99) | copy-start | bytes 772
  225.4 6.0 %copy-start.3 = (f32[1,128,2048]{1,2,0:T(8,128)S(1)}, f32[1,128,2048]{1,2,0:T(8,128)}, u32[]{:S(2)}) copy-start(f32[1,128,2048]{1,2,0:T(8,128)} %copy-done.2) | copy-start | bytes 3145732
  225.4 52.9 %copy-start.1 = (f32[128,32,128]{2,1,0:T(8,128)S(1)}, f32[128,32,128]{2,1,0:T(8,128)}, u32[]{:S(2)}) copy-start(f32[128,32,128]{2,1,0:T(8,128)} %all-gather.21.cloned.1.call-done) | copy-start | bytes 6291460
  278.2 11.7 %copy-start.14 = (f32[1,64,128]{2,1,0:T(8,128)S(1)}, f32[1,64,128]{2,1,0:T(8,128)}, u32[]{:S(2)}) copy-start(f32[1,64,128]{2,1,0:T(8,128)} %param.13) | copy-start | bytes 98308
  292.6 5.4 %copy-start.8 = (bf16[1,128,2048]{1,2,0:T(8,128)(2,1)S(1)}, bf16[1,128,2048]{1,2,0:T(8,128)(2,1)}, u32[]{:S(2)}) copy-start(bf16[1,128,2048]{1,2,0:T(8,128)(2,1)} %copy-done.7) | copy-start | bytes 1572868
  300.0 4.9 %copy-start.15 = (f32[64,1]{1,0:T(8,128)S(1)}, f32[64,1]{1,0:T(8,128)}, u32[]{:S(2)}) copy-start(f32[64,1]{1,0:T(8,128)} %copy.83) | copy-start | bytes 772
  300.0 14.5 %copy-start.11 = (bf16[1,128,2048]{1,2,0:T(8,128)(2,1)S(1)}, bf16[1,128,2048]{1,2,0:T(8,128)(2,1)}, u32[]{:S(2)}) copy-start(bf16[1,128,2048]{1,2,0:T(8,128)(2,1)} %copy-done.10) | copy-start | bytes 1572868
  307.7 18.7 %all-to-all-start.2 = ((f32[8,1,8]{2,1,0:T(1,128)}), f32[8,1,8]{2,1,0:T(1,128)S(1)}, u32[]{:S(2)}, u32[]{:S(2)}) async-start(f32[8,1,8]{2,1,0:T(1,128)} %bitcast.79), calls=%async_computation.2 | async-start | bytes 8192 | tf_op jit(solution)/shard_map/all_to_all | solution.py:56
  314.5 5.8 %copy-start.9 = (bf16[1,128,2048]{1,2,0:T(8,128)(2,1)S(1)}, bf16[1,128,2048]{1,2,0:T(8,128)(2,1)}, u32[]{:S(2)}) copy-start(bf16[1,128,2048]{1,2,0:T(8,128)(2,1)} %copy-done.7) | copy-start | bytes 1572868
  314.5 5.8 %copy-start.12 = (f32[128,64,32]{0,2,1:T(8,128)S(1)}, f32[128,64,32]{0,2,1:T(8,128)}, u32[]{:S(2)}) copy-start(f32[128,64,32]{0,2,1:T(8,128)} %get-tuple-element.119) | copy-start | bytes 3145732
  314.5 5.8 %copy-start.16 = (f32[128,128]{1,0:T(8,128)S(1)}, f32[128,128]{1,0:T(8,128)}, u32[]{:S(2)}) copy-start(f32[128,128]{1,0:T(8,128)} %fusion.78) | copy-start | bytes 196612
  314.5 5.8 %copy-start.17 = (f32[64,128]{1,0:T(8,128)S(1)}, f32[64,128]{1,0:T(8,128)}, u32[]{:S(2)}) copy-start(f32[64,128]{1,0:T(8,128)} %get-tuple-element.84) | copy-start | bytes 98308
  314.5 5.8 %copy-start.18 = (pred[128,128]{1,0:T(8,128)(4,1)S(1)}, pred[128,128]{1,0:T(8,128)(4,1)}, u32[]{:S(2)}) copy-start(pred[128,128]{1,0:T(8,128)(4,1)} %iota_compare_fusion) | copy-start | bytes 49156
  314.5 5.8 %copy-start.23 = (f32[64]{0:T(128)S(1)}, f32[64]{0:T(128)}, u32[]{:S(2)}) copy-start(f32[64]{0:T(128)} %get-tuple-element.89) | copy-start | bytes 772
  320.4 19.2 %copy-start.22 = (f32[8]{0:T(128)S(1)}, f32[8]{0:T(128)}, u32[]{:S(2)}) copy-start(f32[8]{0:T(128)} %reduce_sum.179) | copy-start | bytes 100
  326.4 13.1 %all-to-all-start.1 = ((f32[8,1,8]{2,1,0:T(1,128)}), f32[8,1,8]{2,1,0:T(1,128)S(1)}, u32[]{:S(2)}, u32[]{:S(2)}) async-start(f32[8,1,8]{2,1,0:T(1,128)} %bitcast.78), calls=%async_computation.1 | async-start | bytes 8192 | tf_op jit(solution)/shard_map/all_to_all | solution.py:56
  340.3 15.6 %all-to-all-start.4 = ((f32[32,1,24]{2,1,0:T(1,128)}), f32[32,1,24]{2,1,0:T(1,128)S(1)}, u32[]{:S(2)}, u32[]{:S(2)}) async-start(f32[32,1,24]{2,1,0:T(1,128)} %broadcast_in_dim.71), calls=%async_computation.4 | async-start | bytes 32768 | tf_op jit(solution)/shard_map/all_to_all | solution.py:62
  (5 other events, 13.7 us)
Sparse Core Ops, SparseCore 0:
  29.1 14.9 all-gather.22
  45.9 17.1 all-gather.20
  65.0 51.4 all-gather.16
  118.1 51.1 all-gather.12
  174.2 51.1 all-gather.18
  227.1 51.1 all-gather.14
